TPU v7x, 256 devices: a whole 4x4x8 slice. The times are simulated.
256 devices in a mesh: dp: 4 (over x), blk: 16 (over z_lo, y, core), mp: 4 (over z_hi).
Axes of the slice: x: 4, y: 4, z: 8 (z_hi: 4, z_lo: 2; z = z_hi * 2 + z_lo), core: 2. Of those that a mesh axis runs over, the one named last changes fastest.
Arguments:
- tokens: bfloat16 [16384, 7168], P('dp', ('blk', 'mp')), may hold values from -6 to 6
- trainer_q: float32 [3584, 7168], P(('mp', 'blk'), 'dp'), may hold values from -0.0625 to 0.0625
- kv_pool: bfloat16 [2, 8192, 3584], P(None, ('dp', 'blk'), 'mp')
- prompt_kv: bfloat16 [2, 16384, 3584], P(None, ('dp', 'blk'), 'mp'), may hold values from -15 to 15
- page_table: int32 [64, 64], P(('dp', 'blk')), may hold values from 0 to 127, as said below
- page_count: int32 [64], P(('dp', 'blk')), may hold values from 1 to 64
- prompt_len: int32 [64], P(('dp', 'blk')), may hold values from 64 to 256
Outputs:
- server_q: bfloat16 [3584, 7168], P('mp', 'blk')
- attn_out: bfloat16 [16384, 3584], P(('dp', 'blk'), 'mp')
Inputs may be any that keep to these rules, and one draw needn't show every extreme that they name: `page_table`: the entries of a row are distinct page numbers of the request's group.
All inputs are finite; a program needn't handle non-finite values.
Results may differ from a plain program's by a relative error of at most 0.012.
The roundings to bfloat16 on the way count: a program that leaves them out, or rounds other values in their place, can miss the bound.
Values may be sent and summed in bfloat16 or wider, within the bound.
A program may use at most 128 MiB of HBM per device.

v0:
```python
import jax
import jax.numpy as jnp
from jax import lax
from jax.sharding import PartitionSpec as P

HD = 224
PAGE = 16


def attend_block(softmax_state, query_heads, key_heads, value_heads, key_mask):
    running_max, row_total, weighted = softmax_state
    scores = jnp.einsum(
        "thd,khd->htk", query_heads, key_heads, preferred_element_type=jnp.float32
    ) * HD ** (-0.5)
    scores = jnp.where(key_mask[None], scores, -1e30)
    new_max = jnp.maximum(running_max, jnp.max(scores, axis=2))
    weights = jnp.where(key_mask[None], jnp.exp(scores - new_max[:, :, None]), 0.0)
    factor = jnp.exp(running_max - new_max)
    row_total = row_total * factor + jnp.sum(weights, axis=2)
    weighted = weighted * factor[:, :, None] + jnp.einsum(
        "htk,khd->htd",
        weights.astype(jnp.bfloat16),
        value_heads,
        preferred_element_type=jnp.float32,
    )
    return (new_max, row_total, weighted)


def body(tokens, trainer_q, kv_pool, prompt_kv, page_table, page_count, prompt_len):
    trainer_rows = lax.all_gather(trainer_q.astype(jnp.bfloat16), "dp", axis=1, tiled=True)
    server_q = lax.all_to_all(trainer_rows, "blk", split_axis=1, concat_axis=0, tiled=True)
    features = lax.all_gather(tokens, "mp", axis=1, tiled=True)
    own_rows = features.shape[0] // lax.axis_size("blk")
    head_width = server_q.shape[0]
    token_local = lax.all_to_all(features, "blk", split_axis=0, concat_axis=1, tiled=True)
    queries = jnp.einsum(
        "td,hd->th",
        token_local,
        lax.all_gather(server_q, "blk", axis=1, tiled=True),
        preferred_element_type=jnp.float32,
    )
    queries = queries.astype(jnp.bfloat16)
    head_count = head_width // HD
    query_heads = queries.reshape(own_rows, head_count, HD)
    length = prompt_len[0]
    row_pages = page_table[0]
    live_slots = jnp.arange(row_pages.shape[0], dtype=jnp.int32) < page_count[0]
    row_index = jnp.arange(own_rows, dtype=jnp.int32)
    own_mask = (row_index[None, :] <= row_index[:, None]) & (row_index[None, :] < length)
    softmax_state = (
        jnp.full((head_count, own_rows), -1e30, jnp.float32),
        jnp.zeros((head_count, own_rows), jnp.float32),
        jnp.zeros((head_count, own_rows, HD), jnp.float32),
    )
    softmax_state = attend_block(
        softmax_state,
        query_heads,
        prompt_kv[0].reshape(own_rows, head_count, HD),
        prompt_kv[1].reshape(own_rows, head_count, HD),
        own_mask,
    )
    shard_piece = lax.all_gather(kv_pool, "blk", axis=1, tiled=True)
    key_count = shard_piece.shape[1]
    page_ids = jnp.arange(key_count, dtype=jnp.int32) // PAGE
    page_used = jnp.any((row_pages[None, :] == page_ids[:, None]) & live_slots[None, :], axis=1)
    key_mask = jnp.broadcast_to(page_used[None, :], (own_rows, key_count))
    running_max, row_total, weighted = attend_block(
        softmax_state,
        query_heads,
        shard_piece[0].reshape(key_count, head_count, HD),
        shard_piece[1].reshape(key_count, head_count, HD),
        key_mask,
    )
    mixed = weighted / row_total[:, :, None]
    mixed = jnp.where((row_index < length)[None, :, None], mixed, 0.0)
    mixed = jnp.transpose(mixed, (1, 0, 2)).reshape(own_rows, head_width).astype(jnp.bfloat16)
    return (server_q, mixed)


def solution(mesh):
    in_specs = (
        P("dp", ("blk", "mp")),
        P(("mp", "blk"), "dp"),
        P(None, ("dp", "blk"), "mp"),
        P(None, ("dp", "blk"), "mp"),
        P(("dp", "blk"), None),
        P(("dp", "blk")),
        P(("dp", "blk")),
    )
    out_specs = (P("mp", "blk"), P(("dp", "blk"), "mp"))
    return jax.shard_map(body, mesh=mesh, in_specs=in_specs, out_specs=out_specs, check_vma=False)
```

profile of v0, /device:TPU:1, one launch (start us, length us, event | category | flops | bytes accessed | tf_op | source)
XLA Modules:
  0.0 293.7 jit_solution(181580022779690303)
XLA Ops:
  7.2 0.7 all-gather.4.cloned.1.call-update
  7.9 0.7 all-gather.8.cloned.1.call-update
  8.7 1.0 convert_element_type.18
  9.7 13.0 %all_gather.12 = bf16[56,7168]{1,0:T(8,128)(2,1)S(1)} all-gather(bf16[56,1792]{1,0:T(8,128)(2,1)S(1)} %convert_element_type.18), channel_id=1, replica_groups=mesh['dp'=4,'blk'=16,'mp'=4] {'dp'}, dimensions={1}, use_global_device_ids=true | all-gather | bytes 1003520 | tf_op jit(solution)/shard_map/all_gather | solution.py:30
  22.7 1.1 all_to_all.28
  23.8 0.5 copy.48
  24.3 50.4 %all_to_all.38 = bf16[56,16,448]{2,0,1:T(8,128)(2,1)S(1)} all-to-all(bf16[56,16,448]{2,0,1:T(8,128)(2,1)S(1)} %copy.48), channel_id=1, replica_groups=mesh['dp'=4,'blk'=16,'mp'=4] {'blk'}, dimensions={1} | all-to-all | bytes 1605632 | tf_op jit(solution)/shard_map/all_to_all | solution.py:31
  74.7 1.2 copy.57
  76.0 24.8 %all-gather.4.cloned.1.call-done = bf16[4096,448]{0,1:T(8,128)(2,1)} async-done(((bf16[4096,112]{0,1:T(8,128)(2,1)}), bf16[4096,448]{0,1:T(8,128)(2,1)}) %all-gather.4.cloned.1.call-update) | async-done | bytes 3670032 | tf_op jit(solution)/shard_map/all_gather | solution.py:32
  100.8 4.3 %copy.62 = bf16[56,16,8,256]{3,2,0,1:T(8,128)(2,1)} copy(bf16[56,16,8,256]{3,2,1,0:T(8,128)(2,1)} %bitcast.70) | data formatting | bytes 7340032 | tf_op jit(solution)/shard_map/all_to_all | solution.py:35
  105.1 5.0 %all-to-all-start.1 = ((bf16[16,256,448]{1,2,0:T(8,128)(2,1)}), bf16[16,256,448]{1,2,0:T(8,128)(2,1)}, u32[]{:S(2)}, u32[]{:S(2)}) async-start(bf16[16,256,448]{1,2,0:T(8,128)(2,1)} %bitcast.66), calls=%async_computation.1 | async-start | bytes 7340032 | tf_op jit(solution)/shard_map/all_to_all | solution.py:35
  111.7 0.2 copy.53
  112.3 76.3 %all-gather.8.cloned.1.call-done = bf16[2,2048,896]{2,1,0:T(8,128)(2,1)} async-done(((bf16[2,128,896]{2,1,0:T(8,128)(2,1)}), bf16[2,2048,896]{2,1,0:T(8,128)(2,1)}) %all-gather.8.cloned.1.call-update) | async-done | bytes 7340048 | tf_op jit(solution)/shard_map/all_gather | solution.py:62
  188.6 6.8 %fusion.36 = (bf16[1,2048,896]{2,1,0:T(8,128)(2,1)}, bf16[1,2048,896]{2,1,0:T(8,128)(2,1)}) fusion(bf16[2,2048,896]{2,1,0:T(8,128)(2,1)} %all-gather.8.cloned.1.call-done), kind=kLoop, calls=%fused_computation.51 | loop fusion | bytes 14680064 | tf_op jit(solution)/shard_map/slice | solution.py:70
  195.3 6.2 %copy.55 = bf16[1,2048,896]{1,2,0:T(8,128)(2,1)} copy(bf16[1,2048,896]{2,1,0:T(8,128)(2,1)} %get-tuple-element.14) | data formatting | bytes 7340032 | tf_op jit(solution)/shard_map/slice | solution.py:70
  201.5 6.2 %copy.56 = bf16[1,2048,896]{1,2,0:T(8,128)(2,1)} copy(bf16[1,2048,896]{2,1,0:T(8,128)(2,1)} %get-tuple-element.15) | data formatting | bytes 7340032 | tf_op jit(solution)/shard_map/slice | solution.py:71
  207.7 59.1 %all-gather.6.cloned.1.call-done = bf16[896,7168]{0,1:T(8,128)(2,1)} async-done(((bf16[896,448]{0,1:T(8,128)(2,1)}), bf16[896,7168]{0,1:T(8,128)(2,1)}) %all-gather.6.cloned.1.call-update) | async-done | bytes 12845072 | tf_op jit(solution)/shard_map/all_gather | solution.py:39
  266.8 9.8 %convolution_convert_fusion = bf16[256,896]{1,0:T(8,128)(2,1)S(1)} fusion(bf16[256,7168]{0,1:T(8,128)(2,1)} %bitcast.4, bf16[896,7168]{0,1:T(8,128)(2,1)} %all-gather.6.cloned.1.call-done), kind=kOutput, calls=%fused_computation.17 | convolution fusion | flops 3288563712 | bytes 16973824 | tf_op jit(solution)/shard_map/td,hd->th/dot_general | solution.py:36
  276.8 0.4 fusion.38
  277.2 4.0 %fusion = (f32[4,256]{1,0:T(4,128)S(1)}, f32[4,256,2048]{2,1,0:T(8,128)S(1)}) fusion(pred[2048]{0:T(1024)(128)(4,1)S(1)} %and_reduce_fusion, bf16[256,4,224]{0,2,1:T(8,128)(2,1)S(1)} %bitcast.69, bf16[2048,4,224]{0,2,1:T(8,128)(2,1)} %bitcast.67), kind=kOutput, calls=%fused_computation.2 | convolution fusion | flops 945814528 | bytes 12523520 | tf_op jit(solution)/shard_map/thd,khd->htk/dot_general | solution.py:12
  281.2 2.2 fusion.1
  283.4 2.1 fusion.7
  285.8 0.4 fusion.15
  286.2 1.0 copy.58
  (22 shorter events, 1.2 us)
Async XLA Ops:
  7.2 93.6 %all-gather.4.cloned.1.call-start = ((), (), s32[]{:S(2)}) async-start(), calls=%async_computation.2 | async-start | bytes 4587520 | tf_op jit(solution)/shard_map/all_gather | solution.py:32
  7.9 180.7 %all-gather.8.cloned.1.call-start = ((), (), s32[]{:S(2)}) async-start(), calls=%async_computation.4 | async-start | bytes 7798784 | tf_op jit(solution)/shard_map/all_gather | solution.py:62
  8.6 258.2 %all-gather.6.cloned.1.call-start = ((), (), s32[]{:S(2)}) async-start(), calls=%async_computation.3 | async-start | bytes 13647872 | tf_op jit(solution)/shard_map/all_gather | solution.py:39
  74.7 36.1 %copy-start.1 = (bf16[2,256,896]{2,1,0:T(8,128)(2,1)S(1)}, bf16[2,256,896]{2,1,0:T(8,128)(2,1)}, u32[]{:S(2)}) copy-start(bf16[2,256,896]{2,1,0:T(8,128)(2,1)} %param.10) | copy-start | bytes 2752516
  100.8 11.2 %copy-start.2 = (s32[1,64]{1,0:T(1,128)S(1)}, s32[1,64]{1,0:T(1,128)}, u32[]{:S(2)}) copy-start(s32[1,64]{1,0:T(1,128)} %param.11) | copy-start | bytes 772
  105.1 102.6 %all-to-all-start.1 = ((bf16[16,256,448]{1,2,0:T(8,128)(2,1)}), bf16[16,256,448]{1,2,0:T(8,128)(2,1)}, u32[]{:S(2)}, u32[]{:S(2)}) async-start(bf16[16,256,448]{1,2,0:T(8,128)(2,1)} %bitcast.66), calls=%async_computation.1 | async-start | bytes 7340032 | tf_op jit(solution)/shard_map/all_to_all | solution.py:35
  277.2 6.2 %copy-start = (bf16[1,2048,896]{1,2,0:T(8,128)(2,1)S(1)}, bf16[1,2048,896]{1,2,0:T(8,128)(2,1)}, u32[]{:S(2)}) copy-start(bf16[1,2048,896]{1,2,0:T(8,128)(2,1)} %copy.56) | copy-start | bytes 11010052
Sparse Core Ops, SparseCore 0:
  9.8 90.9 all-gather.3
  102.6 85.9 all-gather.7
  191.0 75.7 all-gather.5
where the time goes:
time: 294 us
  waiting for transfers between devices  162 us (55%)
  blocking collectives  63.4 us (22%)
  local copies, waits for them, and re-layouts  28 us (10%)
  matrix products  16.6 us (6%)
  between operations  15.2 us (5%)
  starting transfers between devices  5.13 us (2%)
  other arithmetic  3.74 us (1%)
    all_gather x1, waiting for transfers between devices, body(): shard_piece = lax.all_gather(kv_pool, 'blk', axis=1, tiled=True)  76.3 us
    all_gather x1, waiting for transfers between devices, body(): lax.all_gather(server_q, 'blk', axis=1, tiled=True)  59.1 us
    all_to_all x1, blocking collectives, body(): lax.all_to_all(trainer_rows, 'blk', split_axis=1, concat_axis=0, tiled=True)  50.4 us
    all_gather x1, waiting for transfers between devices, body(): features = lax.all_gather(tokens, 'mp', axis=1, tiled=True)  24.8 us
    all_gather x1, blocking collectives, body(): lax.all_gather(trainer_q.astype(jnp.bfloat16), 'dp', axis=1, tiled=True)  13 us
    slice x2, local copies, waits for them, and re-layouts, body(): shard_piece[0].reshape(key_count, head_count, HD)  12.9 us
    dot_general x1, matrix products, body(): jnp.einsum('td,hd->th', token_local, lax.all_gather(server_q, 'blk', axis...  9.77 us
    slice x1, local copies, waits for them, and re-layouts, body(): shard_piece[1].reshape(key_count, head_count, HD)  6.2 us
  transfers between devices with their start and end apart: 4, of which 3 were waited for; matrix products, arithmetic and copies ran while one was open for 9% of the time, Pallas kernels for 0%

commit v1 on v0

--- a/solution.py
+++ b/solution.py
@@ -36,7 +36,9 @@
     queries = jnp.einsum(
         "td,hd->th",
         token_local,
-        lax.all_gather(server_q, "blk", axis=1, tiled=True),
+        jnp.concatenate(
+            lax.all_to_all(jnp.stack([server_q] * lax.axis_size("blk")), "blk", 0, 0), axis=1
+        ),
         preferred_element_type=jnp.float32,
     )
     queries = queries.astype(jnp.bfloat16)

time: 294 us -> 405 us (1.38)
  waiting for transfers between devices: 162 us -> 293 us
  blocking collectives: 63.4 us -> 13 us
  starting transfers between devices: 5.13 us -> 24.4 us
  local copies, waits for them, and re-layouts: 28 us -> 34.8 us
    all_gather x1, waiting for transfers between devices: 76.3 us -> 177 us  [body(): shard_piece = lax.all_gather(kv_pool, 'blk', axis=1, tiled=True)]
    all_gather x1 -> x0, waiting for transfers between devices: 59.1 us -> none  [body(): lax.all_gather(server_q, 'blk', axis=1, tiled=True)]
    all_to_all x1 -> x0, blocking collectives: 50.4 us -> none  [body(): lax.all_to_all(trainer_rows, 'blk', split_axis=1, concat_axis=0, tiled=True)]
    all_to_all x1, waiting for transfers between devices: 0.01 us -> 46.9 us  [body(): lax.all_to_all(features, 'blk', split_axis=0, concat_axis=1, tiled=True)]
    all_gather x1, waiting for transfers between devices: 24.8 us -> 68.3 us  [body(): features = lax.all_gather(tokens, 'mp', axis=1, tiled=True)]
    all_to_all x0 -> x2, starting transfers between devices: none -> 19.1 us  [the longest x1 11.1 us: body(): lax.all_to_all(jnp.stack([server_q] * lax.axis_size('blk')), 'blk', 0, 0)]
    another operation x0 -> x1, local copies, waits for them, and re-layouts: none -> 6.38 us  [body(): jnp.stack([server_q] * lax.axis_size('blk'))]
  transfers between devices with their start and end apart: 4 -> 5, of which waited for: 3 -> 3; matrix products, arithmetic and copies ran while one was open for 9% -> 7% of each run, Pallas kernels for 0% -> 0%
where the time goes in v1:
time: 405 us; the launch traced here: 403 us
  waiting for transfers between devices  293 us (72%)
  local copies, waits for them, and re-layouts  34.8 us (9%)
  starting transfers between devices  24.4 us (6%)
  between operations  16.9 us (4%)
  matrix products  16.6 us (4%)
  blocking collectives  13 us (3%)
    all_gather x1, waiting for transfers between devices, body(): shard_piece = lax.all_gather(kv_pool, 'blk', axis=1, tiled=True)  177 us
    all_gather x1, waiting for transfers between devices, body(): features = lax.all_gather(tokens, 'mp', axis=1, tiled=True)  68.3 us
    all_to_all x1, waiting for transfers between devices, body(): lax.all_to_all(features, 'blk', split_axis=0, concat_axis=1, tiled=True)  46.9 us
    all_gather x1, blocking collectives, body(): lax.all_gather(trainer_q.astype(jnp.bfloat16), 'dp', axis=1, tiled=True)  13 us
    slice x2, local copies, waits for them, and re-layouts, body(): shard_piece[0].reshape(key_count, head_count, HD)  13 us
    all_to_all x1, starting transfers between devices, body(): lax.all_to_all(jnp.stack([server_q] * lax.axis_size('blk')), 'blk', 0, 0)  11.1 us
    dot_general x1, matrix products, body(): jnp.einsum('td,hd->th', token_local, jnp.concatenate(lax.all_to_all(jnp.s...  9.77 us
  transfers between devices with their start and end apart: 5, of which 3 were waited for; matrix products, arithmetic and copies ran while one was open for 7% of the time, Pallas kernels for 0%

profile of v1, /device:TPU:1, one launch (start us, length us, event | category | flops | bytes accessed | tf_op | source)
XLA Modules:
  0.0 402.6 jit_solution(17168457145344901552)
XLA Ops:
  8.0 0.7 all-gather.3.cloned.1.call-update
  8.7 1.0 convert_element_type.18
  9.8 13.0 %all_gather.9 = bf16[56,7168]{1,0:T(8,128)(2,1)S(1)} all-gather(bf16[56,1792]{1,0:T(8,128)(2,1)S(1)} %convert_element_type.18), channel_id=1, replica_groups=mesh['dp'=4,'blk'=16,'mp'=4] {'dp'}, dimensions={1}, use_global_device_ids=true | all-gather | bytes 1003520 | tf_op jit(solution)/shard_map/all_gather | solution.py:30
  22.7 1.1 all_to_all.29
  23.8 1.4 copy.29
  25.3 8.1 %all-to-all-start = ((bf16[56,16,448]{2,0,1:T(8,128)(2,1)}), bf16[56,16,448]{2,0,1:T(8,128)(2,1)S(1)}, u32[]{:S(2)}, u32[]{:S(2)}) async-start(bf16[56,16,448]{2,0,1:T(8,128)(2,1)} %copy.29), calls=%async_computation | async-start | bytes 1835008 | tf_op jit(solution)/shard_map/all_to_all | solution.py:31
  33.3 68.3 %all-gather.3.cloned.1.call-done = bf16[4096,448]{0,1:T(8,128)(2,1)} async-done(((bf16[4096,112]{0,1:T(8,128)(2,1)}), bf16[4096,448]{0,1:T(8,128)(2,1)}) %all-gather.3.cloned.1.call-update) | async-done | bytes 3670032 | tf_op jit(solution)/shard_map/all_gather | solution.py:32
  101.6 4.2 %copy.43 = bf16[56,16,8,256]{3,2,0,1:T(8,128)(2,1)} copy(bf16[56,16,8,256]{3,2,1,0:T(8,128)(2,1)} %bitcast.84) | data formatting | bytes 7340032 | tf_op jit(solution)/shard_map/all_to_all | solution.py:35
  105.8 5.0 %all-to-all-start.1 = ((bf16[16,256,448]{1,2,0:T(8,128)(2,1)}), bf16[16,256,448]{1,2,0:T(8,128)(2,1)}, u32[]{:S(2)}, u32[]{:S(2)}) async-start(bf16[16,256,448]{1,2,0:T(8,128)(2,1)} %bitcast.79), calls=%async_computation.1 | async-start | bytes 7340032 | tf_op jit(solution)/shard_map/all_to_all | solution.py:35
  110.8 0.8 copy.38
  111.7 46.9 %all-to-all-done.1 = bf16[16,256,448]{1,2,0:T(8,128)(2,1)} async-done(((bf16[16,256,448]{1,2,0:T(8,128)(2,1)}), bf16[16,256,448]{1,2,0:T(8,128)(2,1)}, u32[]{:S(2)}, u32[]{:S(2)}) %all-to-all-start.1) | async-done | bytes 3670048 | tf_op jit(solution)/shard_map/all_to_all | solution.py:35
  158.5 6.4 %stack.2 = bf16[16,896,448]{1,2,0:T(8,128)(2,1)} broadcast(bf16[896,448]{0,1:T(8,128)(2,1)S(1)} %copy.38), dimensions={1,2} | broadcast | bytes 13647872 | tf_op jit(solution)/shard_map/stack | solution.py:40
  164.9 11.1 %all-to-all-start.2 = ((bf16[16,896,448]{1,2,0:T(8,128)(2,1)}), bf16[16,896,448]{1,2,0:T(8,128)(2,1)}, u32[]{:S(2)}, u32[]{:S(2)}) async-start(bf16[16,896,448]{1,2,0:T(8,128)(2,1)} %stack.2), calls=%async_computation.2 | async-start | bytes 25690112 | tf_op jit(solution)/shard_map/all_to_all | solution.py:40
  178.7 177.0 %all-gather.5.cloned.1.call-done = bf16[2,2048,896]{2,1,0:T(8,128)(2,1)} async-done(((bf16[2,128,896]{2,1,0:T(8,128)(2,1)}), bf16[2,2048,896]{2,1,0:T(8,128)(2,1)}) %all-gather.5.cloned.1.call-update) | async-done | bytes 7340048 | tf_op jit(solution)/shard_map/all_gather | solution.py:64
  355.6 6.8 %fusion.49 = (bf16[1,2048,896]{2,1,0:T(8,128)(2,1)}, bf16[1,2048,896]{2,1,0:T(8,128)(2,1)}) fusion(bf16[2,2048,896]{2,1,0:T(8,128)(2,1)} %all-gather.5.cloned.1.call-done), kind=kLoop, calls=%fused_computation.55 | loop fusion | bytes 14680064 | tf_op jit(solution)/shard_map/slice | solution.py:72
  362.5 6.1 %copy.36 = bf16[1,2048,896]{1,2,0:T(8,128)(2,1)} copy(bf16[1,2048,896]{2,1,0:T(8,128)(2,1)} %get-tuple-element.10) | data formatting | bytes 7340032 | tf_op jit(solution)/shard_map/slice | solution.py:72
  368.6 6.2 %copy.37 = bf16[1,2048,896]{1,2,0:T(8,128)(2,1)} copy(bf16[1,2048,896]{2,1,0:T(8,128)(2,1)} %get-tuple-element.11) | data formatting | bytes 7340032 | tf_op jit(solution)/shard_map/slice | solution.py:73
  374.9 9.8 %fusion.23 = bf16[256,896]{1,0:T(8,128)(2,1)S(1)} fusion(bf16[16,896,448]{1,2,0:T(8,128)(2,1)} %all-to-all-done.2, bf16[16,256,448]{1,2,0:T(8,128)(2,1)} %all-to-all-done.1), kind=kOutput, calls=%fused_computation.21 | convolution fusion | flops 3288563712 | bytes 16973824 | tf_op jit(solution)/shard_map/td,hd->th/dot_general | solution.py:36
  384.8 0.4 fusion.51
  385.2 4.0 fusion.2
  389.2 2.2 fusion.3
  391.4 2.1 fusion.10
  393.8 0.4 fusion.28
  394.2 1.0 copy.39
  (25 shorter events, 1.8 us)
Async XLA Ops:
  8.0 93.6 %all-gather.3.cloned.1.call-start = ((), (), s32[]{:S(2)}) async-start(), calls=%async_computation.3 | async-start | bytes 4587520 | tf_op jit(solution)/shard_map/all_gather | solution.py:32
  25.3 80.6 %all-to-all-start = ((bf16[56,16,448]{2,0,1:T(8,128)(2,1)}), bf16[56,16,448]{2,0,1:T(8,128)(2,1)S(1)}, u32[]{:S(2)}, u32[]{:S(2)}) async-start(bf16[56,16,448]{2,0,1:T(8,128)(2,1)} %copy.29), calls=%async_computation | async-start | bytes 1835008 | tf_op jit(solution)/shard_map/all_to_all | solution.py:31
  105.8 52.7 %all-to-all-start.1 = ((bf16[16,256,448]{1,2,0:T(8,128)(2,1)}), bf16[16,256,448]{1,2,0:T(8,128)(2,1)}, u32[]{:S(2)}, u32[]{:S(2)}) async-start(bf16[16,256,448]{1,2,0:T(8,128)(2,1)} %bitcast.79), calls=%async_computation.1 | async-start | bytes 7340032 | tf_op jit(solution)/shard_map/all_to_all | solution.py:35
  111.6 53.3 %copy-start.1 = (bf16[896,448]{0,1:T(8,128)(2,1)}, bf16[896,448]{0,1:T(8,128)(2,1)S(1)}, u32[]{:S(2)}) copy-start(bf16[896,448]{0,1:T(8,128)(2,1)S(1)} %copy.38) | copy-start | bytes 2408452
  164.9 12.3 %copy-start.2 = (bf16[2,256,896]{2,1,0:T(8,128)(2,1)S(1)}, bf16[2,256,896]{2,1,0:T(8,128)(2,1)}, u32[]{:S(2)}) copy-start(bf16[2,256,896]{2,1,0:T(8,128)(2,1)} %param.10) | copy-start | bytes 2752516
  164.9 13.5 %copy-start.3 = (s32[1,64]{1,0:T(1,128)S(1)}, s32[1,64]{1,0:T(1,128)}, u32[]{:S(2)}) copy-start(s32[1,64]{1,0:T(1,128)} %param.11) | copy-start | bytes 772
  164.9 209.9 %all-to-all-start.2 = ((bf16[16,896,448]{1,2,0:T(8,128)(2,1)}), bf16[16,896,448]{1,2,0:T(8,128)(2,1)}, u32[]{:S(2)}, u32[]{:S(2)}) async-start(bf16[16,896,448]{1,2,0:T(8,128)(2,1)} %stack.2), calls=%async_computation.2 | async-start | bytes 25690112 | tf_op jit(solution)/shard_map/all_to_all | solution.py:40
  176.0 179.7 %all-gather.5.cloned.1.call-start = ((), (), s32[]{:S(2)}) async-start(), calls=%async_computation.4 | async-start | bytes 7798784 | tf_op jit(solution)/shard_map/all_gather | solution.py:64
  385.2 6.2 %copy-start = (bf16[1,2048,896]{1,2,0:T(8,128)(2,1)S(1)}, bf16[1,2048,896]{1,2,0:T(8,128)(2,1)}, u32[]{:S(2)}) copy-start(bf16[1,2048,896]{1,2,0:T(8,128)(2,1)} %copy.37) | copy-start | bytes 11010052
Sparse Core Ops, SparseCore 0:
  10.6 90.9 all-gather.2
Sparse Core Ops, SparseCore 1:
  178.2 177.4 all-gather.4
